TPU v7x, 256 devices: a whole 4x4x8 slice. The times are simulated.
256 devices in a mesh: gen: 8 (over z_lo, core), user: 16 (over x, y), cand: 2 (over z_hi).
Axes of the slice: x: 4, y: 4, z: 8 (z_hi: 2, z_lo: 4; z = z_hi * 4 + z_lo), core: 2. Of those that a mesh axis runs over, the one named last changes fastest.
Arguments:
- states: bfloat16 [16384, 4096], P(('user', 'cand')), may hold values from -6 to 6
- norm_gain: float32 [4096], replicated, may hold values from 0.1 to 1.9
- gate_weight: bfloat16 [4096, 7168], P('user', 'gen'), may hold values from -0.09375 to 0.09375
- up_weight: bfloat16 [4096, 7168], P('user', 'gen'), may hold values from -0.09375 to 0.09375
- down_weight: bfloat16 [7168, 4096], P('gen', 'user'), may hold values from -0.0625 to 0.0625
- proj_weight: bfloat16 [4096, 1024], P('gen'), may hold values from -0.09375 to 0.09375
- private_rows: bfloat16 [32768, 1024], P(('gen', 'user')), may hold values from -6 to 6
- enc_weight: bfloat16 [1024, 1024], replicated, may hold values from -0.1875 to 0.1875
- user_ids: int32 [32768], P(('gen', 'user')), may hold values from 0 to 31
Outputs:
- votes: float32 [16, 2, 128], P(None, 'cand')
Inputs may be any that keep to these rules, and one draw needn't show every extreme that they name: `user_ids`: a user is a pair of a block of 256 rows and a slot; no user has rows in two blocks.
All inputs are finite; a program needn't handle non-finite values.
Results may differ from a plain program's by a relative error of at most 0.0025.
Values may be sent and summed in bfloat16 or wider, within the bound.
No kernel may reach another device: no remote copies, remote signals or barrier semaphores. Data moves between devices by JAX's collectives and lax.ppermute only.
A program may use at most 128 MiB of HBM per device.

v0:
```python
import jax
import jax.numpy as jnp
from jax import lax
from jax.sharding import PartitionSpec as P

STEPS = 4
CAP = 8
USERS_DEV = 32


def unit_rows(matrix):
    return (matrix * lax.rsqrt(jnp.sum(matrix * matrix, axis=1, keepdims=True) + 1e-06)).astype(
        jnp.bfloat16
    )


def project_in(inputs, gate_part, up_part):

    def add_rows(piece):
        return jnp.dot(inputs, piece, preferred_element_type=jnp.float32)

    gate = add_rows(lax.all_gather(gate_part, "user", axis=0, tiled=True))
    up_proj = add_rows(lax.all_gather(up_part, "user", axis=0, tiled=True))
    return (gate, up_proj)


def shards(
    states,
    norm_gain,
    gate_weight,
    up_weight,
    down_weight,
    proj_weight,
    private_rows,
    enc_weight,
    user_ids,
):
    tok_rows, width_model = states.shape
    groups = tok_rows // STEPS
    values = states.astype(jnp.float32)
    normed = (
        values * lax.rsqrt(jnp.mean(values * values, axis=1, keepdims=True) + 1e-05) * norm_gain
    ).astype(jnp.bfloat16)
    gate_part, up_part, down_part = (gate_weight, up_weight, down_weight)
    gate, up_proj = project_in(normed, gate_part, up_part)
    hidden = (jax.nn.silu(gate) * up_proj).astype(jnp.bfloat16)
    mixed = jnp.dot(
        hidden,
        lax.all_gather(down_part, "user", axis=1, tiled=True),
        preferred_element_type=jnp.float32,
    )
    pooled_mlp = jnp.sum(mixed.reshape(-1, STEPS, width_model), axis=1)
    pooled_mlp = lax.psum_scatter(pooled_mlp, "gen", scatter_dimension=1, tiled=True)
    slab_width = pooled_mlp.shape[1]
    own_cols = lax.dynamic_slice_in_dim(values, lax.axis_index("gen") * slab_width, slab_width, 1)
    pooled_in = jnp.sum(own_cols.reshape(groups, STEPS, slab_width), axis=1)
    pooled = ((pooled_in + pooled_mlp) / STEPS).astype(jnp.bfloat16)
    partial_emb = jnp.dot(pooled, proj_weight, preferred_element_type=jnp.float32)
    embedding = lax.psum(partial_emb, "gen")
    candidate = unit_rows(embedding)
    every_cand = lax.all_gather(candidate, "user", axis=0, tiled=True)
    encoded = unit_rows(jnp.dot(private_rows, enc_weight, preferred_element_type=jnp.float32))
    scores = lax.dot_general(
        encoded, every_cand, (((1,), (1,)), ((), ())), preferred_element_type=jnp.float32
    )
    kernel = jnp.exp(scores * 60.0)
    totals = lax.psum(jnp.sum(kernel, axis=1), "cand")
    member = (user_ids[:, None] == jnp.arange(USERS_DEV, dtype=jnp.int32)[None, :]).astype(
        jnp.float32
    )
    counts = jnp.sum(member, axis=0)
    limit = jnp.minimum(1.0, CAP / jnp.maximum(counts, 1.0))
    row_cap = jnp.dot(member, limit, precision=lax.Precision.HIGHEST)
    row_total = private_rows.shape[0] * lax.axis_size("gen") * lax.axis_size("user")
    cand_total = every_cand.shape[0] * lax.axis_size("cand")
    weight_rows = row_cap / totals * (cand_total / row_total)
    partial_votes = jnp.dot(weight_rows, kernel, precision=lax.Precision.HIGHEST)
    votes = lax.psum(partial_votes, ("gen", "user"))
    return votes.reshape(lax.axis_size("user"), 1, groups)


def solution(mesh):
    return jax.shard_map(
        shards,
        mesh=mesh,
        in_specs=(
            P(("user", "cand"), None),
            P(),
            P("user", "gen"),
            P("user", "gen"),
            P("gen", "user"),
            P("gen", None),
            P(("gen", "user"), None),
            P(),
            P(("gen", "user")),
        ),
        out_specs=P(None, "cand", None),
        check_vma=False,
    )
```

profile of v0, /device:TPU:0, one launch (start us, length us, event | category | flops | bytes accessed | tf_op | source)
XLA Modules:
  0.0 810.1 jit_solution(10870717847516051505)
XLA Ops:
  6.5 0.0 copy-start
  6.5 0.0 copy-start.1
  6.5 0.0 all-gather.5.cloned.1.call-start
  6.5 0.7 all-gather.5.cloned.1.call-update
  7.3 0.0 all-gather.7.cloned.1.call-start
  7.3 0.7 all-gather.7.cloned.1.call-update
  8.0 0.0 all-gather.9.cloned.1.call-start
  8.1 0.7 all-gather.9.cloned.1.call-update
  8.7 0.0 reduce-scatter.2.cloned.1.call-start
  8.8 3.1 multiply_reduce_fusion
  11.9 70.3 %all-gather.5.cloned.1.call-done = bf16[4096,896]{1,0:T(8,128)(2,1)} async-done(((bf16[256,896]{1,0:T(8,128)(2,1)}), bf16[4096,896]{1,0:T(8,128)(2,1)}) %all-gather.5.cloned.1.call-update) | async-done | bytes 7340048 | tf_op jit(solution)/shard_map/all_gather | solution.py:22
  82.2 0.0 copy-done.1
  82.2 10.1 %fusion.1 = f32[512,896]{1,0:T(8,128)} fusion(bf16[4096,896]{1,0:T(8,128)(2,1)} %all-gather.5.cloned.1.call-done, f32[4096]{0:T(1024)S(1)} %copy-done.1, f32[512]{0:T(512)S(1)} %add_rsqrt_fusion, bf16[512,4096]{1,0:T(8,128)(2,1)} %param.9), kind=kOutput, calls=%fused_computation.5 | convolution fusion | flops 3766484992 | bytes 13387776 | tf_op jit(solution)/shard_map/dot_general | solution.py:20
  92.3 63.2 %all-gather.7.cloned.1.call-done = bf16[4096,896]{1,0:T(8,128)(2,1)} async-done(((bf16[256,896]{1,0:T(8,128)(2,1)}), bf16[4096,896]{1,0:T(8,128)(2,1)}) %all-gather.7.cloned.1.call-update) | async-done | bytes 7340048 | tf_op jit(solution)/shard_map/all_gather | solution.py:23
  155.6 79.3 %all-gather.9.cloned.1.call-done = bf16[896,4096]{1,0:T(8,128)(2,1)} async-done(((bf16[896,256]{1,0:T(8,128)(2,1)}), bf16[896,4096]{1,0:T(8,128)(2,1)}) %all-gather.9.cloned.1.call-update) | async-done | bytes 7340048 | tf_op jit(solution)/shard_map/all_gather | solution.py:49
  234.8 17.4 %fusion.2 = f32[512,4096]{1,0:T(8,128)} fusion(bf16[896,4096]{1,0:T(8,128)(2,1)} %all-gather.9.cloned.1.call-done, f32[512,896]{1,0:T(8,128)} %fusion.1, bf16[4096,896]{1,0:T(8,128)(2,1)} %all-gather.7.cloned.1.call-done, f32[4096]{0:T(1024)S(1)} %copy-done.1, f32[512]{0:T(512)S(1)} %add_rsqrt_fusion, bf16[512,4096]{1,0:T(8,128)(2,1)} %param.9), kind=kOutput, calls=%fused_computation.9 | convolution fusion | flops 7527333888 | bytes 29116416 | tf_op jit(solution)/shard_map/dot_general | solution.py:47
  252.2 9.8 %reshape.32 = f32[128,4,4096]{2,1,0:T(4,128)} reshape(f32[512,4096]{1,0:T(8,128)} %fusion.2) | data formatting | bytes 16777216 | tf_op jit(solution)/shard_map/reshape | solution.py:52
  262.0 10.0 %reduce_sum.67 = f32[128,4096]{1,0:T(8,128)} reduce(f32[128,4,4096]{2,1,0:T(4,128)} %reshape.32, f32[]{:T(128)} %constant.15.clone.1), dimensions={1}, to_apply=%region_4.5 | reduce | flops 1572864 | bytes 10485764 | tf_op jit(solution)/shard_map/reduce_sum | solution.py:52
  272.0 0.0 reduce-scatter.2.cloned.1.call-update
  272.1 0.0 all-reduce.2.cloned.1.call-start
  272.1 6.5 convert_element_type.23
  278.6 1.3 constant_dynamic-slice_fusion
  279.9 0.0 copy-start.2
  279.9 1.3 reshape.31
  281.2 1.8 reduce_sum.65
  283.1 29.9 %reduce-scatter.2.cloned.1.call-done = f32[128,512]{1,0:T(8,128)} async-done(((f32[128,4096]{1,0:T(8,128)}), f32[128,512]{1,0:T(8,128)}) %reduce-scatter.2.cloned.1.call-update) | async-done | bytes 262160 | tf_op jit(solution)/shard_map/reduce_scatter | solution.py:53
  313.0 2.4 fusion.4
  315.4 0.0 all-reduce.2.cloned.1.call-update
  315.4 0.3 all-gather.11.cloned.1.call-start
  315.7 70.7 %all-reduce.2.cloned.1.call-done = f32[128,1024]{1,0:T(8,128)} async-done(((f32[128,1024]{1,0:T(8,128)}), f32[128,1024]{1,0:T(8,128)}) %all-reduce.2.cloned.1.call-update) | async-done | bytes 524304 | tf_op jit(solution)/shard_map/psum | solution.py:59
  386.3 1.2 multiply_reduce_fusion.2
  387.5 1.8 multiply_convert_fusion.8
  389.3 0.0 all-gather.11.cloned.1.call-update
  389.4 0.0 copy-done.2
  389.4 0.1 convert_reduce_fusion
  389.5 0.0 copy-done
  389.5 1.8 multiply_reduce_fusion.1
  391.3 0.1 fusion.6
  391.5 53.5 %all-gather.11.cloned.1.call-done = bf16[2048,1024]{1,0:T(8,128)(2,1)} async-done(((bf16[128,1024]{1,0:T(8,128)(2,1)}), bf16[2048,1024]{1,0:T(8,128)(2,1)}) %all-gather.11.cloned.1.call-update) | async-done | bytes 4194320 | tf_op jit(solution)/shard_map/all_gather | solution.py:61
  445.0 4.9 fusion.16
  449.8 8.8 %psum.22 = f32[256]{0:T(256)S(1)} all-reduce(f32[256]{0:T(256)S(1)} %get-tuple-element.7), channel_id=1, replica_groups=mesh['gen'=8,'user'=16,'cand'=2] {'cand'}, use_global_device_ids=true, to_apply=%region_9.10 | all-reduce | flops 256 | bytes 2048 | tf_op jit(solution)/shard_map/psum | solution.py:67
  458.6 2.7 convolution_bitcast_fusion
  461.3 341.9 %psum.23 = f32[16,1,128]{2,1,0:T(1,128)} all-reduce(f32[16,1,128]{2,1,0:T(1,128)S(1)} %convolution_bitcast_fusion), channel_id=1, replica_groups=mesh['gen'=8,'user'=16,'cand'=2] {'gen','user'}, use_global_device_ids=true, to_apply=%region_10.11 | all-reduce | flops 2048 | bytes 16384 | tf_op jit(solution)/shard_map/psum | solution.py:78
  (4 shorter events, 0.0 us)
Async XLA Ops:
  6.5 383.0 %copy-start = (bf16[1024,1024]{1,0:T(8,128)(2,1)S(1)}, bf16[1024,1024]{1,0:T(8,128)(2,1)}, u32[]{:S(2)}) copy-start(bf16[1024,1024]{1,0:T(8,128)(2,1)} %param.16) | copy-start | bytes 6291460
  6.5 75.7 %copy-start.1 = (f32[4096]{0:T(1024)S(1)}, f32[4096]{0:T(1024)}, u32[]{:S(2)}) copy-start(f32[4096]{0:T(1024)} %param.10) | copy-start | bytes 49156
  6.5 75.7 %all-gather.5.cloned.1.call-start = ((), (), s32[]{:S(2)}) async-start(), calls=%async_computation.1 | async-start | bytes 7798784 | tf_op jit(solution)/shard_map/all_gather | solution.py:22
  7.3 148.3 %all-gather.7.cloned.1.call-start = ((), (), s32[]{:S(2)}) async-start(), calls=%async_computation.2 | async-start | bytes 7798784 | tf_op jit(solution)/shard_map/all_gather | solution.py:23
  8.0 226.8 %all-gather.9.cloned.1.call-start = ((), (), s32[]{:S(2)}) async-start(), calls=%async_computation.3 | async-start | bytes 7798784 | tf_op jit(solution)/shard_map/all_gather | solution.py:49
  8.7 304.2 %reduce-scatter.2.cloned.1.call-start = ((), (), s32[]{:S(2)}) async-start(), calls=%async_computation.4 | async-start | bytes 2359296 | tf_op jit(solution)/shard_map/reduce_scatter | solution.py:53
  272.1 114.3 %all-reduce.2.cloned.1.call-start = ((), (), s32[]{:S(2)}) async-start(), calls=%async_computation.5 | async-start | bytes 1048576 | tf_op jit(solution)/shard_map/psum | solution.py:59
  279.9 109.5 %copy-start.2 = (s32[256]{0:T(256)S(1)}, s32[256]{0:T(256)}, u32[]{:S(2)}) copy-start(s32[256]{0:T(256)} %param.17) | copy-start | bytes 3076
  315.4 129.5 %all-gather.11.cloned.1.call-start = ((), (), s32[]{:S(2)}) async-start(), calls=%async_computation.6 | async-start | bytes 4456448 | tf_op jit(solution)/shard_map/all_gather | solution.py:61
Sparse Core Ops, SparseCore 0:
  9.8 72.3 all-gather.4
  84.7 70.8 all-gather.6
  158.0 76.7 all-gather.8
  272.2 40.7 reduce-scatter.1
  315.5 70.7 all-reduce.1
  389.5 55.4 all-gather.10
where the time goes:
time: 811 us; the launch traced here: 810 us
  waiting for transfers between devices  369 us (45%)
  blocking collectives  351 us (43%)
  matrix products  39.5 us (5%)
  other arithmetic  24.6 us (3%)
  between operations  13.5 us (2%)
  local copies, waits for them, and re-layouts  12.4 us (2%)
    psum x1, blocking collectives, shards(): votes = lax.psum(partial_votes, ('gen', 'user'))  342 us
    all_gather x1, waiting for transfers between devices, shards(): lax.all_gather(down_part, 'user', axis=1, tiled=True)  79.3 us
    psum x1, waiting for transfers between devices, shards(): embedding = lax.psum(partial_emb, 'gen')  70.7 us
    all_gather x1, waiting for transfers between devices, project_in(): gate = add_rows(lax.all_gather(gate_part, 'user', axis=0, tiled=True))  70.3 us
    all_gather x1, waiting for transfers between devices, project_in(): up_proj = add_rows(lax.all_gather(up_part, 'user', axis=0, tiled=True))  63.2 us
    all_gather x1, waiting for transfers between devices, shards(): every_cand = lax.all_gather(candidate, 'user', axis=0, tiled=True)  53.5 us
    reduce_scatter x1, waiting for transfers between devices, shards(): lax.psum_scatter(pooled_mlp, 'gen', scatter_dimension=1, tiled=True)  29.9 us
    dot_general x1, matrix products, shards(): jnp.dot(hidden, lax.all_gather(down_part, 'user', axis=1, tiled=True), pr...  17.4 us
  transfers between devices with their start and end apart: 6, of which 6 were waited for; matrix products, arithmetic and copies ran while one was open for 3% of the time, Pallas kernels for 0%

commit v1 on v0

--- a/solution.py
+++ b/solution.py
@@ -6,6 +6,13 @@
 STEPS = 4
 CAP = 8
 USERS_DEV = 32
+
+
+def exchange_gather(x, name, d):
+    count = lax.axis_size(name)
+    pieces = jnp.stack([x for _ in range(count)])
+    pieces = lax.all_to_all(pieces, name, split_axis=0, concat_axis=0)
+    return jnp.concatenate(pieces, axis=d)
 
 
 def unit_rows(matrix):
@@ -20,7 +27,7 @@
         return jnp.dot(inputs, piece, preferred_element_type=jnp.float32)
 
     gate = add_rows(lax.all_gather(gate_part, "user", axis=0, tiled=True))
-    up_proj = add_rows(lax.all_gather(up_part, "user", axis=0, tiled=True))
+    up_proj = add_rows(exchange_gather(up_part, "user", 0))
     return (gate, up_proj)
 
 

time: 811 us -> 838 us (1.033)
  waiting for transfers between devices: 369 us -> 386 us
    all_gather x1, waiting for transfers between devices: 70.3 us -> 150 us  [project_in(): gate = add_rows(lax.all_gather(gate_part, 'user', axis=0, tiled=True))]
    all_gather x1 -> x0, waiting for transfers between devices: 63.2 us -> none  [project_in(): up_proj = add_rows(lax.all_gather(up_part, 'user', axis=0, tiled=True))]
  transfers between devices with their start and end apart: 6 -> 6, of which waited for: 6 -> 5; matrix products, arithmetic and copies ran while one was open for 3% -> 4% of each run, Pallas kernels for 0% -> 0%
where the time goes in v1:
time: 838 us; the launch traced here: 837 us
  waiting for transfers between devices  386 us (46%)
  blocking collectives  351 us (42%)
  matrix products  39.4 us (5%)
  other arithmetic  24.7 us (3%)
  local copies, waits for them, and re-layouts  17.4 us (2%)
  between operations  13.2 us (2%)
    psum x1, blocking collectives, shards(): votes = lax.psum(partial_votes, ('gen', 'user'))  342 us
    all_gather x1, waiting for transfers between devices, project_in(): gate = add_rows(lax.all_gather(gate_part, 'user', axis=0, tiled=True))  150 us
    all_gather x1, waiting for transfers between devices, shards(): lax.all_gather(down_part, 'user', axis=1, tiled=True)  80.2 us
    psum x1, waiting for transfers between devices, shards(): embedding = lax.psum(partial_emb, 'gen')  70.7 us
    all_gather x1, waiting for transfers between devices, shards(): every_cand = lax.all_gather(candidate, 'user', axis=0, tiled=True)  53.5 us
    reduce_scatter x1, waiting for transfers between devices, shards(): lax.psum_scatter(pooled_mlp, 'gen', scatter_dimension=1, tiled=True)  29.8 us
    dot_general x1, matrix products, shards(): jnp.dot(hidden, lax.all_gather(down_part, 'user', axis=1, tiled=True), pr...  17.3 us
  transfers between devices with their start and end apart: 6, of which 5 were waited for; matrix products, arithmetic and copies ran while one was open for 4% of the time, Pallas kernels for 0%

profile of v1, /device:TPU:0, one launch (start us, length us, event | category | flops | bytes accessed | tf_op | source)
XLA Modules:
  0.0 837.2 jit_solution(5066370205742171028)
XLA Ops:
  6.5 0.0 copy-start
  6.5 0.0 all-gather.4.cloned.1.call-start
  6.5 0.7 all-gather.4.cloned.1.call-update
  7.3 0.0 all-gather.6.cloned.1.call-start
  7.3 0.7 all-gather.6.cloned.1.call-update
  8.0 5.0 stack.2
  13.1 5.4 all-to-all-start
  18.4 0.0 copy-start.1
  18.4 0.0 reduce-scatter.2.cloned.1.call-start
  18.5 3.1 multiply_reduce_fusion
  21.6 150.2 %all-gather.4.cloned.1.call-done = bf16[4096,896]{1,0:T(8,128)(2,1)} async-done(((bf16[256,896]{1,0:T(8,128)(2,1)}), bf16[4096,896]{1,0:T(8,128)(2,1)}) %all-gather.4.cloned.1.call-update) | async-done | bytes 7340048 | tf_op jit(solution)/shard_map/all_gather | solution.py:29
  171.8 0.0 copy-done.1
  171.8 10.1 %fusion.1 = f32[512,896]{1,0:T(8,128)} fusion(bf16[4096,896]{1,0:T(8,128)(2,1)} %all-gather.4.cloned.1.call-done, f32[4096]{0:T(1024)S(1)} %copy-done.1, f32[512]{0:T(512)S(1)} %add_rsqrt_fusion, bf16[512,4096]{1,0:T(8,128)(2,1)} %param.9), kind=kOutput, calls=%fused_computation.5 | convolution fusion | flops 3766484992 | bytes 13387776 | tf_op jit(solution)/shard_map/dot_general | solution.py:27
  181.9 0.0 all-to-all-done
  181.9 80.2 %all-gather.6.cloned.1.call-done = bf16[896,4096]{1,0:T(8,128)(2,1)} async-done(((bf16[896,256]{1,0:T(8,128)(2,1)}), bf16[896,4096]{1,0:T(8,128)(2,1)}) %all-gather.6.cloned.1.call-update) | async-done | bytes 7340048 | tf_op jit(solution)/shard_map/all_gather | solution.py:56
  262.1 17.3 %fusion.2 = f32[512,4096]{1,0:T(8,128)} fusion(bf16[896,4096]{1,0:T(8,128)(2,1)} %all-gather.6.cloned.1.call-done, f32[512,896]{1,0:T(8,128)} %fusion.1, bf16[4096,896]{1,0:T(8,128)(2,1)} %bitcast.2, f32[4096]{0:T(1024)S(1)} %copy-done.1, f32[512]{0:T(512)S(1)} %add_rsqrt_fusion, bf16[512,4096]{1,0:T(8,128)(2,1)} %param.9), kind=kOutput, calls=%fused_computation.9 | convolution fusion | flops 7527333888 | bytes 29116416 | tf_op jit(solution)/shard_map/dot_general | solution.py:54
  279.4 9.8 %reshape.38 = f32[128,4,4096]{2,1,0:T(4,128)} reshape(f32[512,4096]{1,0:T(8,128)} %fusion.2) | data formatting | bytes 16777216 | tf_op jit(solution)/shard_map/reshape | solution.py:59
  289.2 10.1 %reduce_sum.67 = f32[128,4096]{1,0:T(8,128)} reduce(f32[128,4,4096]{2,1,0:T(4,128)} %reshape.38, f32[]{:T(128)} %constant.15.clone.1), dimensions={1}, to_apply=%region_4.5 | reduce | flops 1572864 | bytes 10485764 | tf_op jit(solution)/shard_map/reduce_sum | solution.py:59
  299.3 0.0 reduce-scatter.2.cloned.1.call-update
  299.3 0.0 all-reduce.2.cloned.1.call-start
  299.4 6.6 convert_element_type.23
  306.0 1.3 constant_dynamic-slice_fusion
  307.3 0.0 copy-start.2
  307.3 1.3 reshape.36
  308.6 1.8 reduce_sum.65
  310.4 29.8 %reduce-scatter.2.cloned.1.call-done = f32[128,512]{1,0:T(8,128)} async-done(((f32[128,4096]{1,0:T(8,128)}), f32[128,512]{1,0:T(8,128)}) %reduce-scatter.2.cloned.1.call-update) | async-done | bytes 262160 | tf_op jit(solution)/shard_map/reduce_scatter | solution.py:60
  340.3 2.4 fusion.4
  342.7 0.0 all-reduce.2.cloned.1.call-update
  342.7 0.3 all-gather.8.cloned.1.call-start
  343.0 70.7 %all-reduce.2.cloned.1.call-done = f32[128,1024]{1,0:T(8,128)} async-done(((f32[128,1024]{1,0:T(8,128)}), f32[128,1024]{1,0:T(8,128)}) %all-reduce.2.cloned.1.call-update) | async-done | bytes 524304 | tf_op jit(solution)/shard_map/psum | solution.py:66
  413.7 1.2 multiply_reduce_fusion.2
  414.9 1.8 multiply_convert_fusion.8
  416.7 0.0 all-gather.8.cloned.1.call-update
  416.8 0.0 copy-done.2
  416.8 0.1 convert_reduce_fusion
  416.9 0.0 copy-done
  416.9 1.8 multiply_reduce_fusion.1
  418.7 0.1 fusion.6
  418.9 53.5 %all-gather.8.cloned.1.call-done = bf16[2048,1024]{1,0:T(8,128)(2,1)} async-done(((bf16[128,1024]{1,0:T(8,128)(2,1)}), bf16[2048,1024]{1,0:T(8,128)(2,1)}) %all-gather.8.cloned.1.call-update) | async-done | bytes 4194320 | tf_op jit(solution)/shard_map/all_gather | solution.py:68
  472.3 4.9 fusion.16
  477.2 8.8 %psum.22 = f32[256]{0:T(256)S(1)} all-reduce(f32[256]{0:T(256)S(1)} %get-tuple-element.7), channel_id=1, replica_groups=mesh['gen'=8,'user'=16,'cand'=2] {'cand'}, use_global_device_ids=true, to_apply=%region_9.10 | all-reduce | flops 256 | bytes 2048 | tf_op jit(solution)/shard_map/psum | solution.py:74
  486.0 2.7 convolution_bitcast_fusion
  488.7 341.9 %psum.23 = f32[16,1,128]{2,1,0:T(1,128)} all-reduce(f32[16,1,128]{2,1,0:T(1,128)S(1)} %convolution_bitcast_fusion), channel_id=1, replica_groups=mesh['gen'=8,'user'=16,'cand'=2] {'gen','user'}, use_global_device_ids=true, to_apply=%region_10.11 | all-reduce | flops 2048 | bytes 16384 | tf_op jit(solution)/shard_map/psum | solution.py:85
  (4 shorter events, 0.0 us)
Async XLA Ops:
  6.5 410.4 %copy-start = (bf16[1024,1024]{1,0:T(8,128)(2,1)S(1)}, bf16[1024,1024]{1,0:T(8,128)(2,1)}, u32[]{:S(2)}) copy-start(bf16[1024,1024]{1,0:T(8,128)(2,1)} %param.16) | copy-start | bytes 6291460
  6.5 165.2 %all-gather.4.cloned.1.call-start = ((), (), s32[]{:S(2)}) async-start(), calls=%async_computation.2 | async-start | bytes 7798784 | tf_op jit(solution)/shard_map/all_gather | solution.py:29
  7.3 254.8 %all-gather.6.cloned.1.call-start = ((), (), s32[]{:S(2)}) async-start(), calls=%async_computation.3 | async-start | bytes 7798784 | tf_op jit(solution)/shard_map/all_gather | solution.py:56
  13.1 168.8 %all-to-all-start = ((bf16[16,256,896]{2,1,0:T(8,128)(2,1)}), bf16[16,256,896]{2,1,0:T(8,128)(2,1)}, u32[]{:S(2)}, u32[]{:S(2)}) async-start(bf16[16,256,896]{2,1,0:T(8,128)(2,1)} %stack.2), calls=%async_computation | async-start | bytes 14680064 | tf_op jit(solution)/shard_map/all_to_all | solution.py:14
  18.4 153.3 %copy-start.1 = (f32[4096]{0:T(1024)S(1)}, f32[4096]{0:T(1024)}, u32[]{:S(2)}) copy-start(f32[4096]{0:T(1024)} %param.10) | copy-start | bytes 49156
  18.4 321.8 %reduce-scatter.2.cloned.1.call-start = ((), (), s32[]{:S(2)}) async-start(), calls=%async_computation.4 | async-start | bytes 2359296 | tf_op jit(solution)/shard_map/reduce_scatter | solution.py:60
  299.3 114.4 %all-reduce.2.cloned.1.call-start = ((), (), s32[]{:S(2)}) async-start(), calls=%async_computation.5 | async-start | bytes 1048576 | tf_op jit(solution)/shard_map/psum | solution.py:66
  307.3 109.5 %copy-start.2 = (s32[256]{0:T(256)S(1)}, s32[256]{0:T(256)}, u32[]{:S(2)}) copy-start(s32[256]{0:T(256)} %param.17) | copy-start | bytes 3076
  342.7 129.6 %all-gather.8.cloned.1.call-start = ((), (), s32[]{:S(2)}) async-start(), calls=%async_computation.6 | async-start | bytes 4456448 | tf_op jit(solution)/shard_map/all_gather | solution.py:68
Sparse Core Ops, SparseCore 0:
  9.8 161.8 all-gather.3
  174.2 87.8 all-gather.5
  299.4 40.7 reduce-scatter.1
  342.8 70.8 all-reduce.1
  416.9 55.4 all-gather.7
